TPU v7x, 32 devices: a whole 2x2x4 slice. The times are simulated.
32 devices in a mesh: dp: 2 (over core), row: 4 (over y, x), col: 4 (over z).
Axes of the slice: x: 2, y: 2, z: 4, core: 2. Of those that a mesh axis runs over, the one named last changes fastest.
Arguments:
- tokens: bfloat16 [256, 8192], P(('dp', 'col'), 'row'), may hold values from -6 to 6
- cotangent: bfloat16 [256, 8192], P(('dp', 'col'), 'row'), may hold values from -6 to 6
- weight: bfloat16 [8192, 16384], P('row', 'col'), may hold values from -0.125 to 0.125
- block_mask: int32 [32, 64], P('row', 'col'), may hold values 0 or 1
Outputs:
- output: bfloat16 [256, 8192], P(('dp', 'col'), 'row')
- input_grad: bfloat16 [256, 8192], P(('dp', 'col'), 'row')
- weight_grad: float32 [8192, 2, 8192], P('row', 'dp', 'col')
Inputs may be any that keep to these rules, and one draw needn't show every extreme that they name: block_mask holds only 0 and 1.
All inputs are finite; a program needn't handle non-finite values. No bound on the sum of `block_mask` on one device may be relied on, other than what follows from the above.
Results may differ from a plain program's by a relative error of at most 0.0032.
Values may be sent and summed in bfloat16 or wider, within the bound.
A program may use at most 128 MiB of HBM per device.

v0:
```python
import math
import jax
import jax.numpy as jnp
from jax import lax
from jax.sharding import PartitionSpec as P

BLOCK = 256


def partner(block, axis, stride):
    count = lax.axis_size(axis)
    route = []
    for low in range(count):
        high = low | 1 << stride
        if high != low and high < count:
            route += [(low, high), (high, low)]
    return lax.ppermute(block, axis, route)


def expand_mask(block_mask):
    kept_blocks = block_mask.astype(jnp.bfloat16)
    return jnp.repeat(jnp.repeat(kept_blocks, BLOCK, axis=0), BLOCK, axis=1)


def slope_times(grad_hidden, pre):
    sigmoid_pre = jax.nn.sigmoid(pre)
    return (grad_hidden * sigmoid_pre * (1.0 + pre * (1.0 - sigmoid_pre))).astype(jnp.bfloat16)


def times_transpose(left, masked):
    return lax.dot_general(
        left, masked, (((1,), (1,)), ((), ())), preferred_element_type=jnp.float32
    )


def on_device(tokens, cotangent, weight, block_mask):
    kept = expand_mask(block_mask)
    masked = weight * kept
    tok_count = tokens.shape[0]
    tok_rows, cot_rows = (
        lax.all_gather(tokens, "col", axis=0, tiled=True),
        lax.all_gather(cotangent, "col", axis=0, tiled=True),
    )
    pre_part = jnp.dot(tok_rows, masked, preferred_element_type=jnp.float32)
    pre = lax.psum(pre_part, "row")
    hidden = jax.nn.silu(pre).astype(jnp.bfloat16)
    grad_part = jnp.dot(cot_rows, masked, preferred_element_type=jnp.float32)
    grad_hidden = lax.psum(grad_part, "row")
    grad_pre = slope_times(grad_hidden, pre)
    projected = lax.psum_scatter(
        times_transpose(hidden, masked), "col", scatter_dimension=0, tiled=True
    )
    output = (tokens.astype(jnp.float32) + projected).astype(jnp.bfloat16)
    back = lax.psum_scatter(
        times_transpose(grad_pre, masked), "col", scatter_dimension=0, tiled=True
    )
    input_grad = (cotangent.astype(jnp.float32) + back).astype(jnp.bfloat16)
    tok_total = tok_count * lax.axis_size("col") * lax.axis_size("dp")
    norm_scale = 1.0 / math.sqrt(tok_total)
    feat_rows = masked.shape[0]
    share_cols = masked.shape[1] // lax.axis_size("dp")
    dp_index = lax.axis_index("dp")
    low_bit = dp_index % 2
    groups = lax.axis_size("dp") // 2
    row_total = hidden.shape[0]
    hid_split = hidden.reshape(row_total, groups, 2, share_cols)
    grad_split = grad_pre.reshape(row_total, groups, 2, share_cols)
    hid_class = lax.dynamic_index_in_dim(hid_split, low_bit, 2, keepdims=False)
    grad_class = lax.dynamic_index_in_dim(grad_split, low_bit, 2, keepdims=False)
    hid_other = lax.dynamic_index_in_dim(hid_split, 1 - low_bit, 2, keepdims=False)
    grad_other = lax.dynamic_index_in_dim(grad_split, 1 - low_bit, 2, keepdims=False)
    other_tok, other_cot, other_hid, other_grad = partner(
        (tok_rows, cot_rows, hid_other, grad_other), "dp", 0
    )
    pair_tok = jnp.concatenate([tok_rows, other_tok], axis=0)
    pair_cot = jnp.concatenate([cot_rows, other_cot], axis=0)
    pair_hid = jnp.concatenate([hid_class, other_hid], axis=0)
    pair_grad = jnp.concatenate([grad_class, other_grad], axis=0)
    partial_value = jnp.einsum(
        "td,tqj->qdj", pair_cot, pair_hid, preferred_element_type=jnp.float32
    )
    partial_value = partial_value + jnp.einsum(
        "td,tqj->qdj", pair_tok, pair_grad, preferred_element_type=jnp.float32
    )
    bit_count = lax.axis_size("dp").bit_length() - 1
    for bit_level in range(bit_count - 1, 0, -1):
        halves = partial_value.reshape(2, partial_value.shape[0] // 2, feat_rows, share_cols)
        my_half = dp_index // 2**bit_level % 2
        keep_part = lax.dynamic_index_in_dim(halves, my_half, 0, keepdims=False)
        send_part = lax.dynamic_index_in_dim(halves, 1 - my_half, 0, keepdims=False)
        partial_value = keep_part + partner(send_part, "dp", bit_level)
    kept_share = lax.dynamic_slice_in_dim(kept, dp_index * share_cols, share_cols, 1)
    summed = partial_value[0] * kept_share.astype(jnp.float32) * norm_scale
    weight_grad = summed.reshape(feat_rows, 1, share_cols)
    return (output, input_grad, weight_grad)


def solution(mesh):
    in_specs = (P(("dp", "col"), "row"), P(("dp", "col"), "row"), P("row", "col"), P("row", "col"))
    out_specs = (P(("dp", "col"), "row"), P(("dp", "col"), "row"), P("row", "dp", "col"))
    return jax.shard_map(
        on_device, mesh=mesh, in_specs=in_specs, out_specs=out_specs, check_vma=False
    )
```

profile of v0, /device:TPU:0, one launch (start us, length us, event | category | flops | bytes accessed | tf_op | source)
XLA Modules:
  0.0 298.0 jit_solution(7271732196159105316)
XLA Ops:
  7.2 0.0 copy-start.4
  7.2 0.0 copy-start.2
  7.2 0.0 copy-start.3
  7.2 0.0 all-reduce.3.cloned.1.call-start
  7.2 22.5 %copy.8 = bf16[2048,4096]{0,1:T(8,128)(2,1)} copy(bf16[2048,4096]{1,0:T(8,128)(2,1)} %param.6) | data formatting | bytes 33554432 | tf_op args[2]
  29.7 0.0 copy-done.4
  29.7 0.1 copy.7
  29.8 0.1 broadcast_in_dim.6
  29.9 0.0 copy-done.2
  30.0 18.0 %all_gather.6 = bf16[128,2048]{1,0:T(8,128)(2,1)} all-gather(bf16[32,2048]{1,0:T(8,128)(2,1)S(1)} %copy-done.2), channel_id=1, replica_groups=mesh['dp'=2,'row'=4,'col'=4] {'col'}, dimensions={0}, use_global_device_ids=true | all-gather | bytes 655360 | tf_op jit(solution)/shard_map/all_gather | solution.py:41
  48.0 0.0 copy-done.3
  48.0 16.4 %all_gather.7 = bf16[128,2048]{1,0:T(8,128)(2,1)S(1)} all-gather(bf16[32,2048]{1,0:T(8,128)(2,1)S(1)} %copy-done.3), channel_id=1, replica_groups=mesh['dp'=2,'row'=4,'col'=4] {'col'}, dimensions={0}, use_global_device_ids=true | all-gather | bytes 655360 | tf_op jit(solution)/shard_map/all_gather | solution.py:42
  64.3 8.7 %bitcast_multiply_fusion.1 = bf16[2048,4096]{0,1:T(8,128)(2,1)S(1)} fusion(bf16[2048,4096]{0,1:T(8,128)(2,1)} %copy.8, bf16[2048,16]{0,1:T(8,128)(2,1)S(1)} %bitcast.49), kind=kLoop, calls=%fused_computation.3 | loop fusion | flops 8388608 | bytes 33619968 | tf_op jit(solution)/shard_map/mul | solution.py:38
  73.0 0.0 copy-start
  73.0 7.5 %convolution_bitcast_fusion.1 = f32[128,4096]{0,1:T(8,128)} fusion(bf16[2048,4096]{0,1:T(8,128)(2,1)S(1)} %bitcast_multiply_fusion.1, bf16[128,2048]{1,0:T(8,128)(2,1)} %all_gather.6), kind=kOutput, calls=%fused_computation.5 | convolution fusion | flops 2147483648 | bytes 19398656 | tf_op jit(solution)/shard_map/dot_general | solution.py:44
  80.6 0.0 copy-done
  80.6 6.1 %convolution_bitcast_fusion = f32[128,4096]{0,1:T(8,128)} fusion(bf16[2048,4096]{0,1:T(8,128)(2,1)S(1)} %bitcast_multiply_fusion.1, bf16[128,2048]{1,0:T(8,128)(2,1)S(1)} %all_gather.7), kind=kOutput, calls=%fused_computation.4 | convolution fusion | flops 2147483648 | bytes 19398656 | tf_op jit(solution)/shard_map/dot_general | solution.py:47
  86.7 0.0 all-reduce.3.cloned.1.call-update
  86.7 0.2 reduce-scatter.3.cloned.1.call-start
  86.9 104.7 %all-reduce.3.cloned.1.call-done = (f32[128,4096]{0,1:T(8,128)}, f32[128,4096]{0,1:T(8,128)}) async-done(((f32[128,4096]{0,1:T(8,128)}, f32[128,4096]{0,1:T(8,128)}), (f32[128,4096]{0,1:T(8,128)}, f32[128,4096]{0,1:T(8,128)})) %all-reduce.3.cloned.1.call-update) | async-done | bytes 4194320 | tf_op jit(solution)/shard_map/psum | solution.py:45
  191.6 3.2 %multiply_convert_fusion = (bf16[128,4096]{0,1:T(8,128)(2,1)S(1)}, bf16[128,4096]{0,1:T(8,128)(2,1)S(1)}) fusion(f32[128,4096]{0,1:T(8,128)} %get-tuple-element.6, f32[128,4096]{0,1:T(8,128)} %get-tuple-element.7), kind=kLoop, calls=%fused_computation.6 | loop fusion | flops 5767168 | bytes 6291456 | tf_op jit(solution)/shard_map/convert_element_type | solution.py:27
  194.8 9.1 %fusion.15 = f32[128,2048]{1,0:T(8,128)} fusion(bf16[128,4096]{0,1:T(8,128)(2,1)S(1)} %get-tuple-element.9, bf16[2048,4096]{0,1:T(8,128)(2,1)} %copy-done), kind=kOutput, calls=%fused_computation.30 | convolution fusion | flops 2147483648 | bytes 18874368 | tf_op jit(solution)/shard_map/dot_general | solution.py:31
  204.0 0.0 reduce-scatter.3.cloned.1.call-update
  204.0 0.0 reduce-scatter.5.cloned.1.call-start
  204.0 0.1 collective-permute-start.3
  204.1 0.5 collective-permute-start.1
  204.6 1.0 dynamic-slice_bitcast_fusion.1
  205.7 0.1 collective-permute-start.2
  205.7 0.9 dynamic-slice_bitcast_fusion.3
  206.6 0.0 copy-start.1
  206.7 0.4 collective-permute-start
  207.1 9.3 %fusion.16 = f32[128,2048]{1,0:T(8,128)} fusion(bf16[128,4096]{0,1:T(8,128)(2,1)S(1)} %get-tuple-element.8, bf16[2048,4096]{0,1:T(8,128)(2,1)} %copy-done), kind=kOutput, calls=%fused_computation.31 | convolution fusion | flops 2147483648 | bytes 18874368 | tf_op jit(solution)/shard_map/dot_general | solution.py:31
  216.4 0.0 reduce-scatter.5.cloned.1.call-update
  216.4 0.0 collective-permute-done.3
  216.5 0.0 collective-permute-done.2
  216.5 0.0 copy-done.1
  216.5 9.9 %fusion.7 = f32[2048,2048]{1,0:T(8,128)} fusion(bf16[128,1,2048]{0,2,1:T(8,128)(2,1)} %collective-permute-done.2, bf16[128,1,2048]{0,2,1:T(8,128)(2,1)S(1)} %copy-done.1, bf16[128,2048]{1,0:T(8,128)(2,1)} %collective-permute-done.3, bf16[128,2048]{1,0:T(8,128)(2,1)} %all_gather.6), kind=kOutput, calls=%fused_computation.16 | convolution fusion | flops 2151677952 | bytes 18874368 | tf_op jit(solution)/shard_map/td,tqj->qdj/dot_general | solution.py:82
  226.3 0.0 collective-permute-done.1
  226.3 0.0 collective-permute-done
  226.4 6.0 %broadcast_in_dim.7 = bf16[2048,16,256]{0,2,1:T(8,128)(2,1)} broadcast(bf16[2048,16]{0,1:T(8,128)(2,1)S(1)} %bitcast.50), dimensions={0,1} | broadcast | bytes 16842752 | tf_op jit(solution)/shard_map/broadcast_in_dim | solution.py:22
  232.4 16.1 %fusion.1 = f32[2048,1,2048]{0,2,1:T(8,128)} fusion(f32[2048,2048]{1,0:T(8,128)} %fusion.7, bf16[2048,4096]{0,1:T(8,128)(2,1)} %bitcast.46, s32[]{:T(128)S(6)} %select_n.22, bf16[128,1,2048]{0,2,1:T(8,128)(2,1)S(1)} %collective-permute-done, bf16[128,1,2048]{0,2,1:T(8,128)(2,1)S(1)} %get-tuple-element.10, bf16[128,2048]{1,0:T(8,128)(2,1)} %collective-permute-done.1, ...), kind=kOutput, calls=%fused_computation.2 | convolution fusion | flops 2168455168 | bytes 44040196 | tf_op jit(solution)/shard_map/td,tqj->qdj/dot_general | solution.py:79
  248.5 39.8 %copy.9 = f32[2048,1,2048]{2,1,0:T(1,128)} copy(f32[2048,1,2048]{0,2,1:T(8,128)} %fusion.1) | data formatting | bytes 33554432
  288.2 0.0 reduce-scatter.3.cloned.1.call-done
  288.2 1.6 add_convert_fusion.1
  289.8 0.0 reduce-scatter.5.cloned.1.call-done
  289.8 1.6 add_convert_fusion
  (2 shorter events, 0.0 us)
Async XLA Ops:
  7.2 22.6 %copy-start.4 = (s32[8,16]{1,0:T(8,128)S(1)}, s32[8,16]{1,0:T(8,128)}, u32[]{:S(2)}) copy-start(s32[8,16]{1,0:T(8,128)} %param.7) | copy-start | bytes 1540
  7.2 22.8 %copy-start.2 = (bf16[32,2048]{1,0:T(8,128)(2,1)S(1)}, bf16[32,2048]{1,0:T(8,128)(2,1)}, u32[]{:S(2)}) copy-start(bf16[32,2048]{1,0:T(8,128)(2,1)} %param.4) | copy-start | bytes 393220
  7.2 40.8 %copy-start.3 = (bf16[32,2048]{1,0:T(8,128)(2,1)S(1)}, bf16[32,2048]{1,0:T(8,128)(2,1)}, u32[]{:S(2)}) copy-start(bf16[32,2048]{1,0:T(8,128)(2,1)} %param.5) | copy-start | bytes 393220
  7.2 184.4 %all-reduce.3.cloned.1.call-start = ((), (), s32[]{:S(2)}) async-start(), calls=%async_computation.4 | async-start | bytes 8388608 | tf_op jit(solution)/shard_map/psum | solution.py:45
  73.0 7.6 %copy-start = (bf16[2048,4096]{0,1:T(8,128)(2,1)}, bf16[2048,4096]{0,1:T(8,128)(2,1)S(1)}, u32[]{:S(2)}) copy-start(bf16[2048,4096]{0,1:T(8,128)(2,1)S(1)} %bitcast_multiply_fusion.1) | copy-start | bytes 50331652
  86.7 201.5 %reduce-scatter.3.cloned.1.call-start = ((), (), s32[]{:S(2)}) async-start(), calls=%async_computation.2 | async-start | bytes 1310720 | tf_op jit(solution)/shard_map/reduce_scatter | solution.py:50
  204.0 85.8 %reduce-scatter.5.cloned.1.call-start = ((), (), s32[]{:S(2)}) async-start(), calls=%async_computation.3 | async-start | bytes 1310720 | tf_op jit(solution)/shard_map/reduce_scatter | solution.py:54
  204.0 12.4 %collective-permute-start.3 = (bf16[128,2048]{1,0:T(8,128)(2,1)}, bf16[128,2048]{1,0:T(8,128)(2,1)}, u32[]{:S(2)}, u32[]{:S(2)}) collective-permute-start(bf16[128,2048]{1,0:T(8,128)(2,1)} %all_gather.6), channel_id=1, source_target_pairs={{0,16},{16,0},{1,17},{17,1},{2,18},{18,2},{3,19},{19,3},{4,20},{20... | collective-permute-start | bytes 1572872 | tf_op jit(solution)/shard_map/ppermute | solution.py:17
  204.1 22.2 %collective-permute-start.1 = (bf16[128,2048]{1,0:T(8,128)(2,1)S(1)}, bf16[128,2048]{1,0:T(8,128)(2,1)}, u32[]{:S(2)}, u32[]{:S(2)}) collective-permute-start(bf16[128,2048]{1,0:T(8,128)(2,1)S(1)} %all_gather.7), channel_id=1, source_target_pairs={{0,16},{16,0},{1,17},{17,1},{2,18},{18,2},{3,19},{19,3},{4,20},{20... | collective-permute-start | bytes 1572872 | tf_op jit(solution)/shard_map/ppermute | solution.py:17
  205.7 10.8 %collective-permute-start.2 = (bf16[128,1,2048]{0,2,1:T(8,128)(2,1)}, bf16[128,1,2048]{0,2,1:T(8,128)(2,1)}, u32[]{:S(2)}, u32[]{:S(2)}) collective-permute-start(bf16[128,1,2048]{0,2,1:T(8,128)(2,1)} %get-tuple-element.13), channel_id=1, source_target_pairs={{0,16},{16,0},{1,17},{17,1},{2,18},{18,2},{3,19},{19,3},{4,20},{20... | collective-permute-start | bytes 1572872 | tf_op jit(solution)/shard_map/ppermute | solution.py:17
  206.6 9.8 %copy-start.1 = (bf16[128,1,2048]{0,2,1:T(8,128)(2,1)S(1)}, bf16[128,1,2048]{0,2,1:T(8,128)(2,1)}, u32[]{:S(2)}) copy-start(bf16[128,1,2048]{0,2,1:T(8,128)(2,1)} %get-tuple-element.12) | copy-start | bytes 1572868
  206.7 19.7 %collective-permute-start = (bf16[128,1,2048]{0,2,1:T(8,128)(2,1)}, bf16[128,1,2048]{0,2,1:T(8,128)(2,1)S(1)}, u32[]{:S(2)}, u32[]{:S(2)}) collective-permute-start(bf16[128,1,2048]{0,2,1:T(8,128)(2,1)} %get-tuple-element.11), channel_id=1, source_target_pairs={{0,16},{16,0},{1,17},{17,1},{2,18},{18,2},{3,19},{19,3},{4,20},{20... | collective-permute-start | bytes 1572872 | tf_op jit(solution)/shard_map/ppermute | solution.py:17
Sparse Core Ops, SparseCore 0:
  86.8 104.7 all-reduce.2
  204.1 27.2 reduce-scatter.2
  233.7 25.7 reduce-scatter.4
where the time goes:
time: 300 us; the launch traced here: 298 us
  waiting for transfers between devices  105 us (35%)
  local copies, waits for them, and re-layouts  70.4 us (23%)
  matrix products  58.1 us (19%)
  blocking collectives  34.4 us (11%)
  other arithmetic  15.1 us (5%)
  between operations  13.9 us (5%)
    psum x1, waiting for transfers between devices, on_device(): pre = lax.psum(pre_part, 'row')  105 us
    unnamed x13, local copies, waits for them, and re-layouts  62.3 us
    dot_general x2, matrix products, times_transpose(): lax.dot_general(left, masked, (((1,), (1,)), ((), ())), preferred_element...  18.5 us
    all_gather x1, blocking collectives, on_device(): lax.all_gather(tokens, 'col', axis=0, tiled=True)  18 us
    all_gather x1, blocking collectives, on_device(): lax.all_gather(cotangent, 'col', axis=0, tiled=True)  16.4 us
    dot_general x1, matrix products, on_device(): jnp.einsum('td,tqj->qdj', pair_cot, pair_hid, preferred_element_type=jnp....  16.1 us
    dot_general x1, matrix products, on_device(): jnp.einsum('td,tqj->qdj', pair_tok, pair_grad, preferred_element_type=jnp...  9.87 us
    mul x1, other arithmetic, on_device(): masked = weight * kept  8.67 us
  transfers between devices with their start and end apart: 7, of which 1 were waited for; matrix products, arithmetic and copies ran while one was open for 28% of the time, Pallas kernels for 0%

commit v1 on v0

--- a/solution.py
+++ b/solution.py
@@ -5,6 +5,14 @@
 from jax.sharding import PartitionSpec as P
 
 BLOCK = 256
+
+
+def connect_the_series(w_in, array_dim):
+    w_in = jnp.moveaxis(w_in, 0, array_dim)
+    q_next = w_in.shape
+    return w_in.reshape(
+        *q_next[:array_dim], q_next[array_dim] * q_next[array_dim + 1], *q_next[array_dim + 2 :]
+    )
 
 
 def partner(block, axis, stride):
@@ -37,8 +45,21 @@
     kept = expand_mask(block_mask)
     masked = weight * kept
     tok_count = tokens.shape[0]
+
+    def find_outputs(buf, axis_name, dim_k):
+        ndev = jax.lax.axis_size(axis_name)
+        row_list = tuple(((at, (at + 1) % ndev) for at in range(ndev)))
+        runs = [buf]
+        while len(runs) < ndev:
+            row_out = jax.lax.ppermute(runs[-1], axis_name, row_list)
+            runs.append(row_out)
+        finding = jax.lax.axis_index(axis_name)
+        odd = jnp.stack(runs)
+        runs = odd[(finding - jnp.arange(ndev)) % ndev]
+        return connect_the_series(runs, dim_k)
+
     tok_rows, cot_rows = (
-        lax.all_gather(tokens, "col", axis=0, tiled=True),
+        find_outputs(tokens, "col", 0),
         lax.all_gather(cotangent, "col", axis=0, tiled=True),
     )
     pre_part = jnp.dot(tok_rows, masked, preferred_element_type=jnp.float32)

time: 300 us -> 306 us (1.020)
  blocking collectives: 34.4 us -> 15.8 us
  local copies, waits for them, and re-layouts: 70.4 us -> 79.4 us
  matrix products: 58.1 us -> 65.3 us
  starting transfers between devices: 1.38 us -> 5.76 us
  waiting for transfers between devices: 105 us -> 109 us
    all_gather x1 -> x0, blocking collectives: 18 us -> none  [on_device(): lax.all_gather(tokens, 'col', axis=0, tiled=True)]
    ppermute x0 -> x3, waiting for transfers between devices: none -> 6.44 us  [find_outputs(): row_out = jax.lax.ppermute(runs[-1], axis_name, row_list)]
    dot_general x1, matrix products: 7.54 us -> 12.9 us  [on_device(): pre_part = jnp.dot(tok_rows, masked, preferred_element_type=jnp.float32)]
    ppermute x0 -> x3, starting transfers between devices: none -> 4.41 us  [find_outputs(): row_out = jax.lax.ppermute(runs[-1], axis_name, row_list)]
    dynamic_slice x0 -> x2, local copies, waits for them, and re-layouts: none -> 4.33 us  [the longest x1 2.17 us: on_device(): lax.dynamic_index_in_dim(grad_split, low_bit, 2, keepdims=False)]
    unnamed x13 -> x17, local copies, waits for them, and re-layouts: 62.3 us -> 65.9 us
  transfers between devices with their start and end apart: 7 -> 10, of which waited for: 1 -> 2; matrix products, arithmetic and copies ran while one was open for 28% -> 43% of each run, Pallas kernels for 0% -> 0%
where the time goes in v1:
time: 306 us; the launch traced here: 304 us
  waiting for transfers between devices  109 us (36%)
  local copies, waits for them, and re-layouts  79.4 us (26%)
  matrix products  65.3 us (21%)
  blocking collectives  15.8 us (5%)
  other arithmetic  15.2 us (5%)
  between operations  13.9 us (5%)
  starting transfers between devices  5.76 us (2%)
    psum x1, waiting for transfers between devices, on_device(): pre = lax.psum(pre_part, 'row')  102 us
    unnamed x17, local copies, waits for them, and re-layouts  65.9 us
    dot_general x2, matrix products, times_transpose(): lax.dot_general(left, masked, (((1,), (1,)), ((), ())), preferred_element...  18.3 us
    dot_general x1, matrix products, on_device(): jnp.einsum('td,tqj->qdj', pair_cot, pair_hid, preferred_element_type=jnp....  16.1 us
    all_gather x1, blocking collectives, on_device(): lax.all_gather(cotangent, 'col', axis=0, tiled=True)  15.8 us
    dot_general x1, matrix products, on_device(): pre_part = jnp.dot(tok_rows, masked, preferred_element_type=jnp.float32)  12.9 us
    dot_general x1, matrix products, on_device(): jnp.einsum('td,tqj->qdj', pair_tok, pair_grad, preferred_element_type=jnp...  9.92 us
    mul x1, other arithmetic, on_device(): masked = weight * kept  8.71 us
  transfers between devices with their start and end apart: 10, of which 2 were waited for; matrix products, arithmetic and copies ran while one was open for 43% of the time, Pallas kernels for 0%

profile of v1, /device:TPU:0, one launch (start us, length us, event | category | flops | bytes accessed | tf_op | source)
XLA Modules:
  0.0 304.0 jit_solution(4438465866569541701)
XLA Ops:
  7.2 0.0 copy-start.4
  7.2 0.0 all-reduce.3.cloned.1.call-start
  7.2 3.1 %collective-permute-start = (bf16[32,2048]{1,0:T(8,128)(2,1)}, bf16[32,2048]{1,0:T(8,128)(2,1)S(1)}, u32[]{:S(2)}, u32[]{:S(2)}) collective-permute-start(bf16[32,2048]{1,0:T(8,128)(2,1)} %param.4), channel_id=1, source_target_pairs={{0,1},{1,2},{2,3},{3,0},{4,5},{5,6},{6,7},{7,4},{8,9},{9,10},{10,1... | collective-permute-start | bytes 393224 | tf_op jit(solution)/shard_map/ppermute | solution.py:54
  10.3 22.4 %copy.12 = bf16[2048,4096]{0,1:T(8,128)(2,1)} copy(bf16[2048,4096]{1,0:T(8,128)(2,1)} %param.6) | data formatting | bytes 33554432 | tf_op args[2]
  32.8 0.0 copy-done.4
  32.8 0.1 copy.11
  32.9 0.1 broadcast_in_dim.7
  33.0 0.0 copy-start.2
  33.0 8.7 %bitcast_multiply_fusion.1 = bf16[2048,4096]{0,1:T(8,128)(2,1)S(1)} fusion(bf16[2048,4096]{0,1:T(8,128)(2,1)} %copy.12, bf16[2048,16]{0,1:T(8,128)(2,1)S(1)} %bitcast.56), kind=kLoop, calls=%fused_computation.4 | loop fusion | flops 8388608 | bytes 33619968 | tf_op jit(solution)/shard_map/mul | solution.py:46
  41.7 0.0 copy-done.2
  41.7 0.0 copy-start
  41.7 15.8 %all_gather.3 = bf16[128,2048]{1,0:T(8,128)(2,1)} all-gather(bf16[32,2048]{1,0:T(8,128)(2,1)S(1)} %copy-done.2), channel_id=1, replica_groups=mesh['dp'=2,'row'=4,'col'=4] {'col'}, dimensions={0}, use_global_device_ids=true | all-gather | bytes 655360 | tf_op jit(solution)/shard_map/all_gather | solution.py:63
  57.5 0.0 copy-start.3
  57.5 0.0 collective-permute-done
  57.5 1.0 collective-permute-start.1
  58.5 8.0 %convolution_bitcast_fusion = f32[128,4096]{1,0:T(8,128)} fusion(bf16[2048,4096]{0,1:T(8,128)(2,1)S(1)} %bitcast_multiply_fusion.1, bf16[128,2048]{1,0:T(8,128)(2,1)} %all_gather.3), kind=kOutput, calls=%fused_computation.5 | convolution fusion | flops 2147483648 | bytes 19398656 | tf_op jit(solution)/shard_map/dot_general | solution.py:68
  66.5 0.0 copy-done
  66.5 0.0 collective-permute-done.1
  66.5 0.3 collective-permute-start.2
  66.8 6.4 %collective-permute-done.2 = bf16[32,2048]{1,0:T(8,128)(2,1)S(1)} collective-permute-done((bf16[32,2048]{1,0:T(8,128)(2,1)S(1)}, bf16[32,2048]{1,0:T(8,128)(2,1)S(1)}, u32[]{:S(2)}, u32[]{:S(2)}) %collective-permute-start.2) | collective-permute-done | bytes 131104 | tf_op jit(solution)/shard_map/ppermute | solution.py:54
  73.3 0.0 copy-done.3
  73.3 0.1 pad_maximum_fusion
  73.3 1.4 gather_fusion
  74.8 12.9 %fusion.17 = f32[128,4096]{1,0:T(8,128)} fusion(bf16[128,2048]{1,0:T(8,128)(2,1)} %bitcast.5, bf16[2048,4096]{0,1:T(8,128)(2,1)} %copy-done), kind=kOutput, calls=%fused_computation.42 | convolution fusion | flops 2147483648 | bytes 19398656 | tf_op jit(solution)/shard_map/dot_general | solution.py:65
  87.7 0.0 all-reduce.3.cloned.1.call-update
  87.7 0.2 reduce-scatter.3.cloned.1.call-start
  87.9 102.3 %all-reduce.3.cloned.1.call-done = (f32[128,4096]{1,0:T(8,128)}, f32[128,4096]{1,0:T(8,128)}) async-done(((f32[128,4096]{1,0:T(8,128)}, f32[128,4096]{1,0:T(8,128)}), (f32[128,4096]{1,0:T(8,128)}, f32[128,4096]{1,0:T(8,128)})) %all-reduce.3.cloned.1.call-update) | async-done | bytes 4194320 | tf_op jit(solution)/shard_map/psum | solution.py:66
  190.2 3.1 %multiply_convert_fusion = (bf16[128,4096]{1,0:T(8,128)(2,1)S(1)}, bf16[128,4096]{1,0:T(8,128)(2,1)S(1)}) fusion(f32[128,4096]{1,0:T(8,128)} %get-tuple-element.9, f32[128,4096]{1,0:T(8,128)} %get-tuple-element.10), kind=kLoop, calls=%fused_computation.6 | loop fusion | flops 5767168 | bytes 6291456 | tf_op jit(solution)/shard_map/convert_element_type | solution.py:35
  193.3 9.1 %fusion.18 = f32[128,2048]{1,0:T(8,128)} fusion(bf16[128,4096]{1,0:T(8,128)(2,1)S(1)} %get-tuple-element.12, bf16[2048,4096]{0,1:T(8,128)(2,1)} %copy-done), kind=kOutput, calls=%fused_computation.43 | convolution fusion | flops 2147483648 | bytes 18874368 | tf_op jit(solution)/shard_map/dot_general | solution.py:39
  202.4 0.0 reduce-scatter.3.cloned.1.call-update
  202.4 0.0 reduce-scatter.5.cloned.1.call-start
  202.5 0.1 collective-permute-start.4
  202.6 0.5 collective-permute-start.6
  203.0 0.8 reshape.85
  203.8 0.8 reshape.87
  204.6 2.2 constant_dynamic-slice_fusion.1
  206.8 1.1 copy.29
  207.9 0.1 collective-permute-start.5
  208.0 1.1 copy.30
  209.2 2.2 constant_dynamic-slice_fusion.3
  211.3 1.1 copy.31
  212.4 0.4 collective-permute-start.3
  212.9 0.3 copy.32
  213.2 0.0 copy-start.1
  213.2 9.2 %fusion.19 = f32[128,2048]{1,0:T(8,128)} fusion(bf16[128,4096]{1,0:T(8,128)(2,1)S(1)} %get-tuple-element.11, bf16[2048,4096]{0,1:T(8,128)(2,1)} %copy-done), kind=kOutput, calls=%fused_computation.44 | convolution fusion | flops 2147483648 | bytes 18874368 | tf_op jit(solution)/shard_map/dot_general | solution.py:39
  222.4 0.0 reduce-scatter.5.cloned.1.call-update
  222.4 0.0 collective-permute-done.6
  222.4 0.0 collective-permute-done.5
  222.4 0.0 copy-done.1
  222.4 9.9 %fusion.7 = f32[2048,2048]{1,0:T(8,128)} fusion(bf16[128,1,2048]{2,0,1:T(8,128)(2,1)} %collective-permute-done.5, bf16[128,1,2048]{2,0,1:T(8,128)(2,1)S(1)} %bitcast.55, bf16[128,2048]{1,0:T(8,128)(2,1)} %collective-permute-done.6, bf16[128,2048]{1,0:T(8,128)(2,1)} %bitcast.5), kind=kOutput, calls=%fused_computation.16 | convolution fusion | flops 2151677952 | bytes 18874368 | tf_op jit(solution)/shard_map/td,tqj->qdj/dot_general | solution.py:103
  232.4 0.0 collective-permute-done.4
  232.4 0.0 collective-permute-done.3
  232.4 6.0 %broadcast_in_dim.8 = bf16[2048,16,256]{0,2,1:T(8,128)(2,1)} broadcast(bf16[2048,16]{0,1:T(8,128)(2,1)S(1)} %bitcast.57), dimensions={0,1} | broadcast | bytes 16842752 | tf_op jit(solution)/shard_map/broadcast_in_dim | solution.py:30
  238.4 16.1 %fusion.1 = f32[2048,1,2048]{0,2,1:T(8,128)} fusion(f32[2048,2048]{1,0:T(8,128)} %fusion.7, bf16[2048,4096]{0,1:T(8,128)(2,1)} %bitcast.53, s32[]{:T(128)S(6)} %select_n.47, bf16[128,1,2048]{2,0,1:T(8,128)(2,1)S(1)} %collective-permute-done.3, bf16[128,1,2048]{2,0,1:T(8,128)(2,1)S(1)} %bitcast.54, bf16[128,2048]{1,0:T(8,128)(2,1)} %collective-permute-done.4, ...), kind=kOutput, calls=%fused_computation.3 | convolution fusion | flops 2168455168 | bytes 44040196 | tf_op jit(solution)/shard_map/td,tqj->qdj/dot_general | solution.py:100
  254.5 39.7 %copy.18 = f32[2048,1,2048]{2,1,0:T(1,128)} copy(f32[2048,1,2048]{0,2,1:T(8,128)} %fusion.1) | data formatting | bytes 33554432
  294.2 0.0 reduce-scatter.3.cloned.1.call-done
  294.2 1.6 add_convert_fusion.1
  295.9 0.0 reduce-scatter.5.cloned.1.call-done
  295.9 1.6 add_convert_fusion
  (4 shorter events, 0.0 us)
Async XLA Ops:
  7.2 25.6 %copy-start.4 = (s32[8,16]{1,0:T(8,128)S(1)}, s32[8,16]{1,0:T(8,128)}, u32[]{:S(2)}) copy-start(s32[8,16]{1,0:T(8,128)} %param.7) | copy-start | bytes 1540
  7.2 183.0 %all-reduce.3.cloned.1.call-start = ((), (), s32[]{:S(2)}) async-start(), calls=%async_computation.4 | async-start | bytes 8388608 | tf_op jit(solution)/shard_map/psum | solution.py:66
  7.2 50.3 %collective-permute-start = (bf16[32,2048]{1,0:T(8,128)(2,1)}, bf16[32,2048]{1,0:T(8,128)(2,1)S(1)}, u32[]{:S(2)}, u32[]{:S(2)}) collective-permute-start(bf16[32,2048]{1,0:T(8,128)(2,1)} %param.4), channel_id=1, source_target_pairs={{0,1},{1,2},{2,3},{3,0},{4,5},{5,6},{6,7},{7,4},{8,9},{9,10},{10,1... | collective-permute-start | bytes 393224 | tf_op jit(solution)/shard_map/ppermute | solution.py:54
  33.0 8.7 %copy-start.2 = (bf16[32,2048]{1,0:T(8,128)(2,1)S(1)}, bf16[32,2048]{1,0:T(8,128)(2,1)}, u32[]{:S(2)}) copy-start(bf16[32,2048]{1,0:T(8,128)(2,1)} %param.5) | copy-start | bytes 393220
  41.7 24.8 %copy-start = (bf16[2048,4096]{0,1:T(8,128)(2,1)}, bf16[2048,4096]{0,1:T(8,128)(2,1)S(1)}, u32[]{:S(2)}) copy-start(bf16[2048,4096]{0,1:T(8,128)(2,1)S(1)} %bitcast_multiply_fusion.1) | copy-start | bytes 50331652
  57.5 15.8 %copy-start.3 = (bf16[32,2048]{1,0:T(8,128)(2,1)S(1)}, bf16[32,2048]{1,0:T(8,128)(2,1)}, u32[]{:S(2)}) copy-start(bf16[32,2048]{1,0:T(8,128)(2,1)} %param.4) | copy-start | bytes 393220
  57.5 9.0 %collective-permute-start.1 = (bf16[32,2048]{1,0:T(8,128)(2,1)S(1)}, bf16[32,2048]{1,0:T(8,128)(2,1)S(1)}, u32[]{:S(2)}, u32[]{:S(2)}) collective-permute-start(bf16[32,2048]{1,0:T(8,128)(2,1)S(1)} %collective-permute-done), channel_id=1, source_target_pairs={{0,1},{1,2},{2,3},{3,0},{4,5},{5,6},{6,7},{7,4},{8,9},{9,10},{10,1... | collective-permute-start | bytes 393224 | tf_op jit(solution)/shard_map/ppermute | solution.py:54
  66.5 6.8 %collective-permute-start.2 = (bf16[32,2048]{1,0:T(8,128)(2,1)S(1)}, bf16[32,2048]{1,0:T(8,128)(2,1)S(1)}, u32[]{:S(2)}, u32[]{:S(2)}) collective-permute-start(bf16[32,2048]{1,0:T(8,128)(2,1)S(1)} %collective-permute-done.1), channel_id=1, source_target_pairs={{0,1},{1,2},{2,3},{3,0},{4,5},{5,6},{6,7},{7,4},{8,9},{9,10},{10,1... | collective-permute-start | bytes 393224 | tf_op jit(solution)/shard_map/ppermute | solution.py:54
  87.7 206.5 %reduce-scatter.3.cloned.1.call-start = ((), (), s32[]{:S(2)}) async-start(), calls=%async_computation.2 | async-start | bytes 1310720 | tf_op jit(solution)/shard_map/reduce_scatter | solution.py:71
  202.4 93.5 %reduce-scatter.5.cloned.1.call-start = ((), (), s32[]{:S(2)}) async-start(), calls=%async_computation.3 | async-start | bytes 1310720 | tf_op jit(solution)/shard_map/reduce_scatter | solution.py:75
  202.5 29.9 %collective-permute-start.4 = (bf16[128,2048]{1,0:T(8,128)(2,1)}, bf16[128,2048]{1,0:T(8,128)(2,1)}, u32[]{:S(2)}, u32[]{:S(2)}) collective-permute-start(bf16[128,2048]{1,0:T(8,128)(2,1)} %all_gather.3), channel_id=1, source_target_pairs={{0,16},{16,0},{1,17},{17,1},{2,18},{18,2},{3,19},{19,3},{4,20},{20... | collective-permute-start | bytes 1572872 | tf_op jit(solution)/shard_map/ppermute | solution.py:25
  202.6 19.8 %collective-permute-start.6 = (bf16[128,2048]{1,0:T(8,128)(2,1)}, bf16[128,2048]{1,0:T(8,128)(2,1)}, u32[]{:S(2)}, u32[]{:S(2)}) collective-permute-start(bf16[128,2048]{1,0:T(8,128)(2,1)} %bitcast.5), channel_id=1, source_target_pairs={{0,16},{16,0},{1,17},{17,1},{2,18},{18,2},{3,19},{19,3},{4,20},{20... | collective-permute-start | bytes 1572872 | tf_op jit(solution)/shard_map/ppermute | solution.py:25
  207.9 14.5 %collective-permute-start.5 = (bf16[128,1,2048]{2,0,1:T(8,128)(2,1)}, bf16[128,1,2048]{2,0,1:T(8,128)(2,1)}, u32[]{:S(2)}, u32[]{:S(2)}) collective-permute-start(bf16[128,1,2048]{2,0,1:T(8,128)(2,1)} %bitcast.49), channel_id=1, source_target_pairs={{0,16},{16,0},{1,17},{17,1},{2,18},{18,2},{3,19},{19,3},{4,20},{20... | collective-permute-start | bytes 1572872 | tf_op jit(solution)/shard_map/ppermute | solution.py:25
  212.4 19.9 %collective-permute-start.3 = (bf16[128,1,2048]{2,0,1:T(8,128)(2,1)}, bf16[128,1,2048]{2,0,1:T(8,128)(2,1)S(1)}, u32[]{:S(2)}, u32[]{:S(2)}) collective-permute-start(bf16[128,1,2048]{2,0,1:T(8,128)(2,1)} %bitcast.51), channel_id=1, source_target_pairs={{0,16},{16,0},{1,17},{17,1},{2,18},{18,2},{3,19},{19,3},{4,20},{20... | collective-permute-start | bytes 1572872 | tf_op jit(solution)/shard_map/ppermute | solution.py:25
  213.2 9.3 %copy-start.1 = (bf16[128,1,1,2048]{3,0,2,1:T(8,128)(2,1)S(1)}, bf16[128,1,1,2048]{3,0,2,1:T(8,128)(2,1)}, u32[]{:S(2)}) copy-start(bf16[128,1,1,2048]{3,0,2,1:T(8,128)(2,1)} %copy.30) | copy-start | bytes 1572868
Sparse Core Ops, SparseCore 0:
  87.8 102.3 all-reduce.2
  202.5 27.2 reduce-scatter.2
  232.2 25.7 reduce-scatter.4
